TPU v7x, 32 devices: a whole 2x2x4 slice. The times are simulated.
32 devices in a mesh: tp: 4 (over y, core), ad: 8 (over z, x).
Axes of the slice: x: 2, y: 2, z: 4, core: 2. Of those that a mesh axis runs over, the one named last changes fastest.
Arguments:
- hidden: bfloat16 [2048, 8192], P('ad'), may hold values from -6 to 6
- key_value_weight: bfloat16 [8192, 2048], P(None, 'tp'), may hold values from -0.0625 to 0.0625
- request_group: int32 [2048, 1], P('ad'), may hold values from 0 to 7; in each aligned block of 256 rows (0 to 255, 256 to 511, ...) at most 64 rows name the same one
- request_member: int32 [2048], P('ad'), may hold values from 0 to 3
- adapter_down_weight: bfloat16 [8192, 2048], P('tp', 'ad'), may hold values from -0.0625 to 0.0625
- adapter_up_weight: bfloat16 [2048, 2048], P('ad', 'tp'), may hold values from -0.75 to 0.75
Outputs:
- kv_out: bfloat16 [2048, 2048], P('ad', 'tp')
Inputs may be any that keep to these rules, and one draw needn't show every extreme that they name: `request_group`: among the 256 rows of one index of ad, no group is named by more than 64 rows, a bound that some block reaches.
All inputs are finite; a program needn't handle non-finite values.
Results may differ from a plain program's by a relative error of at most 0.007.
Values may be sent and summed in bfloat16 or wider, within the bound.
No kernel may reach another device: no remote copies, remote signals or barrier semaphores. Data moves between devices by JAX's collectives and lax.ppermute only.
A program may use at most 128 MiB of HBM per device.

v0:
```python
import jax
import jax.numpy as jnp
from jax import lax
from jax.sharding import PartitionSpec as P

ADAPTER_RANK = 64


def shards(
    hidden, key_value_weight, request_group, request_member, adapter_down_weight, adapter_up_weight
):
    column_portion = adapter_down_weight.shape[0]
    adapter_pool_count = adapter_down_weight.shape[1] // ADAPTER_RANK
    base_output = jnp.dot(hidden, key_value_weight, preferred_element_type=jnp.float32)
    own_cols = lax.dynamic_slice_in_dim(
        hidden, lax.axis_index("tp") * column_portion, column_portion, 1
    )
    owner_index = request_group[:, 0]
    adapter = owner_index * adapter_pool_count + request_member
    block_portion = lax.all_gather(adapter_down_weight, "ad", axis=1, tiled=True)
    column_total = block_portion.shape[1]
    scores = jnp.dot(own_cols, block_portion, preferred_element_type=jnp.float32)
    column = jnp.arange(column_total, dtype=jnp.int32)
    kept_mask = (column // ADAPTER_RANK)[None, :] == adapter[:, None]
    selector = (
        (column % ADAPTER_RANK)[:, None] == jnp.arange(ADAPTER_RANK, dtype=jnp.int32)[None, :]
    ).astype(jnp.float32)
    partial_ranks = jnp.dot(
        jnp.where(kept_mask, scores, 0.0), selector, precision=lax.Precision.HIGHEST
    )
    rank_values = lax.psum(partial_ranks, "tp").astype(jnp.bfloat16)
    block_portion = lax.all_gather(adapter_up_weight, "ad", axis=0, tiled=True)
    line_total = block_portion.shape[0]
    row_index = jnp.arange(line_total, dtype=jnp.int32)
    spread = (
        (row_index % ADAPTER_RANK)[None, :] == jnp.arange(ADAPTER_RANK, dtype=jnp.int32)[:, None]
    ).astype(jnp.bfloat16)
    widened = jnp.dot(rank_values, spread, preferred_element_type=jnp.float32)
    kept_mask = (row_index // ADAPTER_RANK)[None, :] == adapter[:, None]
    raised_output = jnp.where(kept_mask, widened, 0.0).astype(jnp.bfloat16)
    adapter_update = jnp.dot(
        raised_output, block_portion, preferred_element_type=jnp.float32
    ).astype(jnp.bfloat16)
    return (base_output + adapter_update.astype(jnp.float32)).astype(jnp.bfloat16)


def solution(mesh):
    placed = (P("ad", None), P(None, "tp"), P("ad", None), P("ad"), P("tp", "ad"), P("ad", "tp"))
    return jax.shard_map(
        shards, mesh=mesh, in_specs=placed, out_specs=P("ad", "tp"), check_vma=False
    )
```

profile of v0, /device:TPU:0, one launch (start us, length us, event | category | flops | bytes accessed | tf_op | source)
XLA Modules:
  0.0 203.6 jit_solution(13971514790394120517)
XLA Ops:
  6.5 0.0 all-gather.3.cloned.1.call-start
  6.5 0.7 all-gather.3.cloned.1.call-update
  7.3 0.0 all-gather.5.cloned.1.call-start
  7.3 0.7 all-gather.5.cloned.1.call-update
  8.0 0.7 broadcast_multiply_fusion
  8.7 0.7 add.34
  9.4 127.7 %all-gather.3.cloned.1.call-done = bf16[2048,2048]{1,0:T(8,128)(2,1)} async-done(((bf16[2048,256]{1,0:T(8,128)(2,1)}), bf16[2048,2048]{1,0:T(8,128)(2,1)}) %all-gather.3.cloned.1.call-update) | async-done | bytes 8388624 | tf_op jit(solution)/shard_map/all_gather | solution.py:20
  137.1 6.1 %compare_select_fusion = f32[256,2048]{1,0:T(8,128)S(1)} fusion(bf16[2048,2048]{1,0:T(8,128)(2,1)} %all-gather.3.cloned.1.call-done, bf16[256,8192]{1,0:T(8,128)(2,1)} %param.6, s32[]{:T(128)S(6)} %select_n.40, s32[2048]{0:T(1024)S(1)} %get-tuple-element.6, s32[256]{0:T(256)S(1)} %add.34), kind=kOutput, calls=%fused_computation.1 | convolution fusion | flops 2148532224 | bytes 11543556 | tf_op jit(solution)/shard_map/dot_general | solution.py:22
  143.1 1.2 fusion.9
  144.4 12.5 %psum.7 = bf16[256,64]{1,0:T(8,128)(2,1)S(1)} all-reduce(f32[256,64]{1,0:T(8,128)S(1)} %fusion.9), channel_id=1, replica_groups=mesh['tp'=4,'ad'=8] {'tp'}, use_global_device_ids=true, to_apply=%region_0.1 | all-reduce | flops 16384 | bytes 98304 | tf_op jit(solution)/shard_map/psum | solution.py:31
  156.9 29.6 %all-gather.5.cloned.1.call-done = bf16[2048,512]{1,0:T(8,128)(2,1)} async-done(((bf16[256,512]{1,0:T(8,128)(2,1)}), bf16[2048,512]{1,0:T(8,128)(2,1)}) %all-gather.5.cloned.1.call-update) | async-done | bytes 2097168 | tf_op jit(solution)/shard_map/all_gather | solution.py:32
  186.5 2.6 %fusion.4 = f32[256,512]{1,0:T(8,128)S(1)} fusion(bf16[2048,512]{1,0:T(8,128)(2,1)} %all-gather.5.cloned.1.call-done, s32[2048]{0:T(1024)S(1)} %get-tuple-element.6, s32[256]{0:T(256)S(1)} %add.34, s32[2048]{0:T(1024)S(1)} %get-tuple-element.5, bf16[256,64]{1,0:T(8,128)(2,1)S(1)} %psum.7), kind=kOutput, calls=%fused_computation.7 | convolution fusion | flops 605945856 | bytes 2671616 | tf_op jit(solution)/shard_map/dot_general | solution.py:41
  189.1 7.7 %fusion.2 = bf16[256,512]{1,0:T(8,128)(2,1)} fusion(f32[256,512]{1,0:T(8,128)S(1)} %fusion.4, bf16[256,8192]{1,0:T(8,128)(2,1)} %param.6, bf16[8192,512]{1,0:T(8,128)(2,1)} %param.7), kind=kOutput, calls=%fused_computation.5 | convolution fusion | flops 2147745792 | bytes 13369344 | tf_op jit(solution)/shard_map/dot_general | solution.py:14
  (1 shorter events, 0.0 us)
Async XLA Ops:
  6.5 130.5 %all-gather.3.cloned.1.call-start = ((), (), s32[]{:S(2)}) async-start(), calls=%async_computation | async-start | bytes 9437184 | tf_op jit(solution)/shard_map/all_gather | solution.py:20
  7.3 179.2 %all-gather.5.cloned.1.call-start = ((), (), s32[]{:S(2)}) async-start(), calls=%async_computation.1 | async-start | bytes 2359296 | tf_op jit(solution)/shard_map/all_gather | solution.py:32
Sparse Core Ops, SparseCore 0:
  9.4 127.6 all-gather.2
  139.2 47.2 all-gather.4
where the time goes:
time: 204 us
  waiting for transfers between devices  159 us (78%)
  matrix products  17.5 us (9%)
  between operations  13.4 us (7%)
  blocking collectives  12.5 us (6%)
    all_gather x1, waiting for transfers between devices, shards(): lax.all_gather(adapter_down_weight, 'ad', axis=1, tiled=True)  128 us
    all_gather x1, waiting for transfers between devices, shards(): block_portion = lax.all_gather(adapter_up_weight, 'ad', axis=0, tiled=True)  29.6 us
    psum x1, blocking collectives, shards(): rank_values = lax.psum(partial_ranks, 'tp').astype(jnp.bfloat16)  12.5 us
    dot_general x1, matrix products, shards(): jnp.dot(hidden, key_value_weight, preferred_element_type=jnp.float32)  7.69 us
    dot_general x1, matrix products, shards(): jnp.dot(own_cols, block_portion, preferred_element_type=jnp.float32)  6.06 us
  transfers between devices with their start and end apart: 2, of which 2 were waited for; matrix products, arithmetic and copies ran while one was open for 4% of the time, Pallas kernels for 0%

commit v1 on v0

--- a/solution.py
+++ b/solution.py
@@ -1,9 +1,17 @@
+import functools
 import jax
 import jax.numpy as jnp
 from jax import lax
 from jax.sharding import PartitionSpec as P
 
 ADAPTER_RANK = 64
+
+
+def _group_wall(mat, across):
+    return jnp.concatenate(lax.all_gather(mat, across), axis=1)
+
+
+report_works = functools.partial(_group_wall, across="ad")
 
 
 def shards(
@@ -17,7 +25,7 @@
     )
     owner_index = request_group[:, 0]
     adapter = owner_index * adapter_pool_count + request_member
-    block_portion = lax.all_gather(adapter_down_weight, "ad", axis=1, tiled=True)
+    block_portion = report_works(adapter_down_weight)
     column_total = block_portion.shape[1]
     scores = jnp.dot(own_cols, block_portion, preferred_element_type=jnp.float32)
     column = jnp.arange(column_total, dtype=jnp.int32)

time: 204 us -> 204 us (level)
  local copies, waits for them, and re-layouts: 0 us -> 11.5 us
  waiting for transfers between devices: 159 us -> 148 us
    reshape x0 -> x1, local copies, waits for them, and re-layouts: none -> 11.5 us  [_group_wall(): return jnp.concatenate(lax.all_gather(mat, across), axis=1)]
    all_gather x1, waiting for transfers between devices: 29.6 us -> 19.6 us  [shards(): block_portion = lax.all_gather(adapter_up_weight, 'ad', axis=0, tiled=True)]
  transfers between devices with their start and end apart: 2 -> 2, of which waited for: 2 -> 2; matrix products, arithmetic and copies ran while one was open for 4% -> 10% of each run, Pallas kernels for 0% -> 0%
where the time goes in v1:
time: 204 us; the launch traced here: 203 us
  waiting for transfers between devices  148 us (73%)
  matrix products  17.9 us (9%)
  between operations  13.4 us (7%)
  local copies, waits for them, and re-layouts  11.5 us (6%)
  blocking collectives  10.8 us (5%)
    all_gather x1, waiting for transfers between devices, _group_wall(): return jnp.concatenate(lax.all_gather(mat, across), axis=1)  127 us
    all_gather x1, waiting for transfers between devices, shards(): block_portion = lax.all_gather(adapter_up_weight, 'ad', axis=0, tiled=True)  19.6 us
    reshape x1, local copies, waits for them, and re-layouts, _group_wall(): return jnp.concatenate(lax.all_gather(mat, across), axis=1)  11.5 us
    psum x1, blocking collectives, shards(): rank_values = lax.psum(partial_ranks, 'tp').astype(jnp.bfloat16)  10.8 us
    dot_general x1, matrix products, shards(): jnp.dot(hidden, key_value_weight, preferred_element_type=jnp.float32)  7.69 us
    dot_general x1, matrix products, shards(): jnp.dot(own_cols, block_portion, preferred_element_type=jnp.float32)  6.11 us
  transfers between devices with their start and end apart: 2, of which 2 were waited for; matrix products, arithmetic and copies ran while one was open for 10% of the time, Pallas kernels for 0%

profile of v1, /device:TPU:0, one launch (start us, length us, event | category | flops | bytes accessed | tf_op | source)
XLA Modules:
  0.0 203.2 jit_solution(7432913187687295518)
XLA Ops:
  6.5 0.0 all-gather.6.cloned.1.call-start
  6.5 0.7 all-gather.6.cloned.1.call-update
  7.3 0.0 all-gather.4.cloned.1.call-start
  7.3 0.7 all-gather.4.cloned.1.call-update
  8.0 0.7 broadcast_multiply_fusion
  8.7 0.7 add.34
  9.4 127.3 %all-gather.6.cloned.1.call-done = bf16[16384,256]{1,0:T(8,128)(2,1)} async-done(((bf16[2048,256]{1,0:T(8,128)(2,1)}), bf16[16384,256]{1,0:T(8,128)(2,1)}) %all-gather.6.cloned.1.call-update) | async-done | bytes 8388624 | tf_op jit(solution)/shard_map/all_gather | solution.py:11
  136.7 11.5 %copy.7 = bf16[2048,8,256]{0,2,1:T(8,128)(2,1)} copy(bf16[2048,8,256]{2,0,1:T(8,128)(2,1)} %bitcast.11) | data formatting | bytes 16777216 | tf_op jit(solution)/shard_map/reshape | solution.py:11
  148.2 6.1 %compare_select_fusion = f32[256,2048]{1,0:T(8,128)S(1)} fusion(bf16[2048,2048]{0,1:T(8,128)(2,1)} %bitcast.12, bf16[256,8192]{1,0:T(8,128)(2,1)} %param.6, s32[]{:T(128)S(6)} %select_n.40, s32[2048]{0:T(1024)S(1)} %get-tuple-element.6, s32[256]{0:T(256)S(1)} %add.34), kind=kOutput, calls=%fused_computation.1 | convolution fusion | flops 2148532224 | bytes 11543556 | tf_op jit(solution)/shard_map/dot_general | solution.py:30
  154.3 1.5 fusion.9
  155.8 10.8 %psum.7 = bf16[256,64]{0,1:T(8,128)(2,1)S(1)} all-reduce(f32[256,64]{0,1:T(8,128)S(1)} %fusion.9), channel_id=1, replica_groups=mesh['tp'=4,'ad'=8] {'tp'}, use_global_device_ids=true, to_apply=%region_0.1 | all-reduce | flops 16384 | bytes 98304 | tf_op jit(solution)/shard_map/psum | solution.py:39
  166.5 19.6 %all-gather.4.cloned.1.call-done = bf16[2048,512]{1,0:T(8,128)(2,1)} async-done(((bf16[256,512]{1,0:T(8,128)(2,1)}), bf16[2048,512]{1,0:T(8,128)(2,1)}) %all-gather.4.cloned.1.call-update) | async-done | bytes 2097168 | tf_op jit(solution)/shard_map/all_gather | solution.py:40
  186.1 2.6 %fusion.4 = f32[256,512]{1,0:T(8,128)S(1)} fusion(bf16[2048,512]{1,0:T(8,128)(2,1)} %all-gather.4.cloned.1.call-done, s32[2048]{0:T(1024)S(1)} %get-tuple-element.6, s32[256]{0:T(256)S(1)} %add.34, s32[2048]{0:T(1024)S(1)} %get-tuple-element.5, bf16[256,64]{0,1:T(8,128)(2,1)S(1)} %psum.7), kind=kOutput, calls=%fused_computation.7 | convolution fusion | flops 605945856 | bytes 2671616 | tf_op jit(solution)/shard_map/dot_general | solution.py:49
  188.7 7.7 %fusion.2 = bf16[256,512]{1,0:T(8,128)(2,1)} fusion(f32[256,512]{1,0:T(8,128)S(1)} %fusion.4, bf16[256,8192]{1,0:T(8,128)(2,1)} %param.6, bf16[8192,512]{1,0:T(8,128)(2,1)} %param.7), kind=kOutput, calls=%fused_computation.5 | convolution fusion | flops 2147745792 | bytes 13369344 | tf_op jit(solution)/shard_map/dot_general | solution.py:22
  (1 shorter events, 0.0 us)
Async XLA Ops:
  6.5 130.1 %all-gather.6.cloned.1.call-start = ((), (), s32[]{:S(2)}) async-start(), calls=%async_computation.1 | async-start | bytes 9437184 | tf_op jit(solution)/shard_map/all_gather | solution.py:11
  7.3 178.9 %all-gather.4.cloned.1.call-start = ((), (), s32[]{:S(2)}) async-start(), calls=%async_computation | async-start | bytes 2359296 | tf_op jit(solution)/shard_map/all_gather | solution.py:40
Sparse Core Ops, SparseCore 0:
  9.5 127.1 all-gather.5
  138.8 47.2 all-gather.3
